TPU v7x, 512 devices: a whole 4x8x8 slice. The times are simulated.
512 devices in a mesh: dp: 8 (over y_hi, core), expert: 64 (over z, x, y_lo).
Axes of the slice: x: 4, y: 8 (y_hi: 4, y_lo: 2; y = y_hi * 2 + y_lo), z: 8, core: 2. Of those that a mesh axis runs over, the one named last changes fastest.
Arguments:
- tokens: bfloat16 [65536, 3584], P(('dp', 'expert')), may hold values from -6 to 6
- cotangent: bfloat16 [65536, 3584], P(('dp', 'expert')), may hold values from -0.59765625 to 0.59765625
- route_ids: int32 [65536, 8], P(('dp', 'expert')), may hold values from 0 to 383, as said below
- gates: bfloat16 [65536, 8], P(('dp', 'expert')), may hold values from 0.099609375 to 1
- w_gate: bfloat16 [64, 3584, 128], P('expert', None, 'dp'), may hold values from -0.09375 to 0.09375
- w_up: bfloat16 [64, 3584, 128], P('expert', None, 'dp'), may hold values from -0.09375 to 0.09375
- w_down: bfloat16 [64, 3584, 128], P('expert', None, 'dp'), may hold values from -0.125 to 0.125
Outputs:
- relaid_gate: bfloat16 [64, 3584, 128], P('expert', 'dp')
- relaid_up: bfloat16 [64, 3584, 128], P('expert', 'dp')
- relaid_down: bfloat16 [64, 3584, 128], P('expert', 'dp')
- grad_gate: float32 [64, 3584, 128], P('expert', 'dp')
- grad_up: float32 [64, 3584, 128], P('expert', 'dp')
- grad_down: float32 [64, 3584, 128], P('expert', 'dp')
- token_grad: bfloat16 [65536, 3584], P(('dp', 'expert'))
- gate_grad: float32 [65536, 8], P(('dp', 'expert'))
Inputs may be any that keep to these rules, and one draw needn't show every extreme that they name: `route_ids`: each row names 8 different experts. Among the 128 rows of one device, at most 6 routes name any one expert below 4; on every device of one index of dp, one same expert below 4 is named by exactly 6 routes.
All inputs are finite; a program needn't handle non-finite values.
Results may differ from a plain program's by a relative error of at most 0.02.
Values may be sent and summed in bfloat16 or wider, within the bound.
No kernel may reach another device: no remote copies, remote signals or barrier semaphores. Data moves between devices by JAX's collectives and lax.ppermute only.
A program may use at most 128 MiB of HBM per device.

v0:
```python
import jax
import jax.numpy as jnp
from jax import lax
from jax.sharding import Mesh
from jax.sharding import PartitionSpec as P

HSPLIT = 16
CAP = 6
PAD = 8
EXPERTS = 4
LANES = 128
DP = ("yh", "core")
BF = jnp.bfloat16
F32 = jnp.float32


def spread(block, axes):
    count = lax.axis_size(axes)
    copies = jnp.broadcast_to(block[None], (count,) + block.shape)
    got = lax.all_to_all(copies, axes, split_axis=0, concat_axis=0, tiled=True)
    return got.reshape((count * block.shape[0],) + block.shape[1:])


def dot(eq, a, b):
    return jnp.einsum(eq, a, b, preferred_element_type=F32)


def shards(tokens, cotangent, route_ids, gates, w_gate, w_up, w_down):
    tok_count, features = tokens.shape
    hidden_dev = w_gate.shape[2]
    mine = jnp.concatenate([w_gate[0].T, w_up[0].T, w_down[0].T], axis=0)
    gathered = lax.all_gather(mine, DP, axis=0, tiled=True)
    n_dp = lax.axis_size(DP)
    ids = route_ids.T
    gates_t = gates.T.astype(F32)
    experts = jnp.arange(EXPERTS, dtype=jnp.int32)
    hits = ids[None] == experts[:, None, None]
    token_hit = jnp.any(hits, axis=1)
    before = (jnp.arange(tok_count)[:, None] < jnp.arange(tok_count)[None, :]).astype(BF)
    rank = dot("et,tu->eu", token_hit.astype(BF), before)
    slots = jnp.arange(PAD, dtype=jnp.int32)
    pick = token_hit[:, None, :] & (rank.astype(jnp.int32)[:, None, :] == slots[None, :, None])
    gate_of = jnp.sum(jnp.where(hits, gates_t[None], 0.0), axis=1)
    gate_slots = jnp.sum(jnp.where(pick, gate_of[:, None, :], 0.0), axis=2)
    pick_rows = pick.reshape(EXPERTS * PAD, tok_count).astype(BF)
    tok_slots = dot("ct,td->cd", pick_rows, tokens).astype(BF)
    cot_slots = dot("ct,td->cd", pick_rows, cotangent).astype(BF)
    gate_cols = jnp.broadcast_to(gate_slots.astype(BF).reshape(-1, 1), (EXPERTS * PAD, LANES))
    rows = jnp.concatenate([tok_slots, gate_cols, cot_slots], axis=1)
    rows = rows.reshape(EXPERTS, PAD, -1)
    rows = lax.all_to_all(rows, "ex", split_axis=0, concat_axis=0, tiled=True)
    rows = rows.reshape(EXPERTS * PAD, -1)
    kept = jnp.arange(EXPERTS * CAP)
    keep = ((kept // CAP * PAD + kept % CAP)[:, None] == jnp.arange(EXPERTS * PAD)[None, :]).astype(
        BF
    )
    wide = features + LANES
    tok_rows = dot("kc,cd->kd", keep, rows[:, :wide]).astype(BF)
    cot_rows = dot("kc,cd->kd", keep, rows[:, wide:]).astype(BF)
    block = EXPERTS * CAP
    tok_half = lax.all_gather(tok_rows, "x", axis=0, tiled=True)
    cot_half = spread(cot_rows, ("zl", "yl"))
    cot_half, gathered = lax.optimization_barrier((cot_half, gathered))
    slot_all = spread(tok_half, ("zl", "yl"))
    slot_cotan = lax.all_gather(cot_half, "x", axis=0, tiled=True)
    slot_tokens = slot_all[:, :features]
    gathered = gathered.reshape(n_dp, 3, hidden_dev, features)

    def reorder(values):
        v = values.reshape(4, 4, block, values.shape[-1])
        return jnp.swapaxes(v, 0, 1).reshape(values.shape)

    slab = [gathered[:, j].reshape(n_dp * hidden_dev, features) for j in range(3)]
    gate_slab, up_slab, down_slab = slab
    pre_gate = reorder(dot("rd,hd->rh", slot_tokens, gate_slab))
    pre_up = reorder(dot("rd,hd->rh", slot_tokens, up_slab))
    slot_gates = reorder(slot_all[:, features : features + 1]).astype(F32)
    sigmoid_gate = jax.nn.sigmoid(pre_gate)
    activation = pre_gate * sigmoid_gate
    hidden = (activation * pre_up).astype(BF)
    back_proj = dot("rd,hd->rh", slot_cotan, down_slab)
    score = jnp.sum(hidden.astype(F32) * back_proj, axis=1, keepdims=True).astype(BF)
    scaled = slot_gates * back_proj
    d_gate = (scaled * pre_up * sigmoid_gate * (1.0 + pre_gate * (1.0 - sigmoid_gate))).astype(BF)
    d_up = (scaled * activation).astype(BF)
    hidden_gated = (slot_gates * hidden.astype(F32)).astype(BF)
    grads = jnp.stack(
        [
            dot("rd,rh->dh", slot_tokens, reorder(d_gate)).astype(BF).reshape(n_dp, -1, LANES),
            dot("rd,rh->dh", slot_tokens, reorder(d_up)).astype(BF).reshape(n_dp, -1, LANES),
            dot("rd,rh->dh", slot_cotan, hidden_gated).astype(BF).reshape(n_dp, -1, LANES),
        ],
        axis=1,
    )
    grads = lax.psum_scatter(grads, DP, scatter_dimension=0, tiled=True)[0].astype(F32)
    left = jnp.concatenate([d_gate, d_up, jnp.broadcast_to(score, d_up.shape)], axis=1)
    first = (jnp.arange(LANES) == 0).astype(BF)[:, None]
    right = jnp.concatenate(
        [
            jnp.concatenate([gate_slab, jnp.zeros((LANES, LANES), BF)], axis=1),
            jnp.concatenate([up_slab, jnp.zeros((LANES, LANES), BF)], axis=1),
            jnp.concatenate(
                [jnp.zeros((LANES, features), BF), jnp.broadcast_to(first, (LANES, LANES))], axis=1
            ),
        ],
        axis=0,
    )
    right = lax.optimization_barrier(right)
    back = dot("rh,hd->rd", left, right).astype(BF)
    back = back.reshape(8, 2 * block, wide)
    back = lax.all_to_all(back, ("x", "zl"), split_axis=0, concat_axis=0, tiled=True)
    back = back.reshape(HSPLIT * block, wide)
    row = jnp.arange(2 * block)
    target = (row // CAP % EXPERTS * 2 + row // block) * PAD + row % CAP
    fold = (jnp.arange(2 * EXPERTS * PAD)[:, None] == target[None, :]).astype(BF)
    home = dot("ck,kd->cd", jnp.tile(fold, (1, 8)), back).astype(BF)
    home = lax.all_to_all(
        home.reshape(2 * EXPERTS, PAD, wide), ("ex", "yl"), split_axis=0, concat_axis=0, tiled=True
    ).reshape(2 * EXPERTS * PAD, wide)
    pick_home = jnp.broadcast_to(pick[:, None], (EXPERTS, 2, PAD, tok_count))
    pick_home = pick_home.reshape(2 * EXPERTS * PAD, tok_count).astype(BF)
    token_grad = dot("ct,cd->td", pick_home, home[:, :features]).astype(BF)
    score_slots = jnp.sum(
        home[:, features : features + 1].astype(F32).reshape(EXPERTS, 2, PAD, 1), axis=1
    )
    score_token = jnp.sum(jnp.where(pick, score_slots, 0.0), axis=1)
    gate_grad = jnp.sum(jnp.where(hits, score_token[:, None, :], 0.0), axis=0).T
    start = lax.axis_index(DP) * (features // n_dp)
    relaid = [lax.dynamic_slice_in_dim(w, start, features // n_dp, axis=1).T[None] for w in slab]
    return (*relaid, grads[0:1], grads[1:2], grads[2:3], token_grad, gate_grad)


def solution(mesh):
    fine = Mesh(mesh.devices.reshape(4, 2, 4, 2, 4, 2), ("yh", "core", "ex", "zl", "x", "yl"))
    expert = ("ex", "zl", "x", "yl")
    rows = P(DP + expert, None)
    weights = P(expert, None, DP)
    laid = P(expert, DP, None)
    return jax.shard_map(
        shards,
        mesh=fine,
        in_specs=(rows,) * 4 + (weights,) * 3,
        out_specs=(laid,) * 6 + (rows,) * 2,
        check_vma=False,
    )
```

profile of v0, /device:TPU:17, one launch (start us, length us, event | category | flops | bytes accessed | tf_op | source)
XLA Modules:
  0.0 203.4 jit_solution(5433098685010183178)
XLA Ops:
  7.2 1.9 pad_maximum_fusion.1
  11.9 1.5 convolution_convert_fusion.6
  14.3 10.0 %all-to-all-start = ((bf16[4,8,7296]{2,1,0:T(8,128)(2,1)}), bf16[4,8,7296]{2,1,0:T(8,128)(2,1)S(1)}, u32[]{:S(2)}, u32[]{:S(2)}) async-start(bf16[4,8,7296]{2,1,0:T(8,128)(2,1)} %maximum_bitcast_fusion), calls=%async_computation | async-start | bytes 933888 | tf_op jit(solution)/shard_map/all_to_all | solution.py:51
  24.3 10.8 %all-to-all-done = bf16[4,8,7296]{2,1,0:T(8,128)(2,1)S(1)} async-done(((bf16[4,8,7296]{2,1,0:T(8,128)(2,1)}), bf16[4,8,7296]{2,1,0:T(8,128)(2,1)S(1)}, u32[]{:S(2)}, u32[]{:S(2)}) %all-to-all-start) | async-done | bytes 466976 | tf_op jit(solution)/shard_map/all_to_all | solution.py:51
  35.4 0.9 broadcast_in_dim.56
  36.3 7.7 %all-to-all-start.1 = ((bf16[4,24,3584]{2,1,0:T(8,128)(2,1)}), bf16[4,24,3584]{2,1,0:T(8,128)(2,1)S(1)}, u32[]{:S(2)}, u32[]{:S(2)}) async-start(bf16[4,24,3584]{2,1,0:T(8,128)(2,1)} %broadcast_in_dim.56), calls=%async_computation.1 | async-start | bytes 1376256 | tf_op jit(solution)/shard_map/all_to_all | solution.py:20
  44.2 12.8 %all_gather.10 = bf16[96,3712]{1,0:T(8,128)(2,1)S(1)} all-gather(bf16[24,3712]{1,0:T(8,128)(2,1)S(1)} %convolution_convert_fusion.7), channel_id=1, replica_groups=mesh['yh'=4,'core'=2,'ex'=4,'zl'=2,'x'=4,'yl'=2] {'x'}, dimensions={0}, use_global_device_ids=true | all-gather | bytes 890880 | tf_op jit(solution)/shard_map/all_gather | solution.py:61
  57.0 5.6 %all-to-all-done.1 = bf16[4,24,3584]{2,1,0:T(8,128)(2,1)S(1)} async-done(((bf16[4,24,3584]{2,1,0:T(8,128)(2,1)}), bf16[4,24,3584]{2,1,0:T(8,128)(2,1)S(1)}, u32[]{:S(2)}, u32[]{:S(2)}) %all-to-all-start.1) | async-done | bytes 688160 | tf_op jit(solution)/shard_map/all_to_all | solution.py:20
  62.6 1.8 broadcast_in_dim.64
  64.5 4.6 %all-to-all-start.2 = ((bf16[4,96,3712]{2,1,0:T(8,128)(2,1)}), bf16[4,96,3712]{2,1,0:T(8,128)(2,1)}, u32[]{:S(2)}, u32[]{:S(2)}) async-start(bf16[4,96,3712]{2,1,0:T(8,128)(2,1)} %broadcast_in_dim.64), calls=%async_computation.2 | async-start | bytes 5701632 | tf_op jit(solution)/shard_map/all_to_all | solution.py:20
  69.8 2.8 %fusion.68 = (bf16[8,1,16,3584]{3,2,1,0:T(8,128)(2,1)}, bf16[8,1,16,3584]{3,2,1,0:T(8,128)(2,1)S(1)}, bf16[8,1,16,3584]{3,2,1,0:T(8,128)(2,1)S(1)}) fusion(bf16[8,3,16,3584]{3,2,1,0:T(8,128)(2,1)} %bitcast.154), kind=kLoop, calls=%fused_computation.125 | loop fusion | bytes 5505024 | tf_op jit(solution)/shard_map/slice | solution.py:73
  72.8 6.1 %fusion.9 = bf16[384,3712]{1,0:T(8,128)(2,1)} fusion(bf16[128,128]{1,0:T(8,128)(2,1)S(1)} %broadcast_in_dim.108, bf16[128,3584]{1,0:T(8,128)(2,1)S(1)} %bitcast.147, bf16[128,3584]{1,0:T(8,128)(2,1)S(1)} %bitcast.150), kind=kLoop, calls=%fused_computation.23 | loop fusion | flops 19955712 | bytes 4718592 | tf_op jit(solution)/shard_map/concatenate | solution.py:98
  78.9 22.7 %all-to-all-done.2 = bf16[4,96,3712]{2,1,0:T(8,128)(2,1)} async-done(((bf16[4,96,3712]{2,1,0:T(8,128)(2,1)}), bf16[4,96,3712]{2,1,0:T(8,128)(2,1)}, u32[]{:S(2)}, u32[]{:S(2)}) %all-to-all-start.2) | async-done | bytes 2850848 | tf_op jit(solution)/shard_map/all_to_all | solution.py:20
  101.6 2.0 slice.65
  103.5 0.9 convolution_bitcast_fusion.2
  104.4 0.9 convolution_bitcast_fusion.1
  105.3 1.0 convert_reduce_fusion
  106.6 7.3 %all-gather.5.cloned.1.call-done = bf16[384,3584]{1,0:T(8,128)(2,1)} async-done(((bf16[96,3584]{1,0:T(8,128)(2,1)}), bf16[384,3584]{1,0:T(8,128)(2,1)}) %all-gather.5.cloned.1.call-update) | async-done | bytes 2752528 | tf_op jit(solution)/shard_map/all_gather | solution.py:65
  113.8 3.0 %fusion.21 = (bf16[384]{0:T(512)(128)(2,1)S(1)}, bf16[384,128]{1,0:T(8,128)(2,1)S(1)}, bf16[384,128]{1,0:T(8,128)(2,1)S(1)}, bf16[384,128]{1,0:T(8,128)(2,1)S(1)}) fusion(f32[4,4,24,128]{3,2,1,0:T(8,128)S(1)} %copy.51, f32[4,4,24,128]{3,2,1,0:T(8,128)S(1)} %copy.52, f32[384]{0:T(512)S(1)} %reshape.223, bf16[384,3584]{1,0:T(8,128)(2,1)} %all-gather.5.cloned.1.call-done, ...), kind=kOutput, calls=%fused_computation.46 | convolution fusion | flops 353255040 | bytes 4360448 | tf_op jit(solution)/shard_map/rd,hd->rh/dot_general | solution.py:25
  116.8 3.8 %convolution_convert_fusion.3 = bf16[3584,128]{1,0:T(8,128)(2,1)} fusion(bf16[384,128]{1,0:T(8,128)(2,1)S(1)} %bitcast.170, bf16[384,3712]{1,0:T(8,128)(2,1)} %bitcast.23), kind=kOutput, calls=%fused_computation.13 | convolution fusion | flops 352780288 | bytes 3768320 | tf_op jit(solution)/shard_map/rd,rh->dh/dot_general | solution.py:25
  120.7 3.2 %convolution_convert_fusion = bf16[384,3712]{1,0:T(8,128)(2,1)} fusion(bf16[384,3712]{1,0:T(8,128)(2,1)S(1)} %copy-done.1, bf16[384,128]{1,0:T(8,128)(2,1)S(1)} %broadcast_in_dim.107, bf16[384,128]{1,0:T(8,128)(2,1)S(1)} %get-tuple-element.53, bf16[384,128]{1,0:T(8,128)(2,1)S(1)} %get-tuple-element.52), kind=kOutput, calls=%fused_computation.10 | convolution fusion | flops 1097023488 | bytes 5996544 | tf_op jit(solution)/shard_map/rh,hd->rd/dot_general | solution.py:25
  124.0 4.4 %all-to-all-start.3 = ((bf16[8,48,3712]{2,1,0:T(8,128)(2,1)}), bf16[8,48,3712]{2,1,0:T(8,128)(2,1)}, u32[]{:S(2)}, u32[]{:S(2)}) async-start(bf16[8,48,3712]{2,1,0:T(8,128)(2,1)} %bitcast.146), calls=%async_computation.4 | async-start | bytes 5701632 | tf_op jit(solution)/shard_map/all_to_all | solution.py:111
  128.6 2.8 %convolution_convert_fusion.2 = bf16[3584,128]{1,0:T(8,128)(2,1)S(1)} fusion(bf16[384,3584]{1,0:T(8,128)(2,1)} %all-gather.5.cloned.1.call-done, bf16[384,128]{1,0:T(8,128)(2,1)S(1)} %get-tuple-element.45, f32[384]{0:T(512)S(1)} %reshape.223), kind=kOutput, calls=%fused_computation.12 | convolution fusion | flops 352927744 | bytes 3769856 | tf_op jit(solution)/shard_map/rd,rh->dh/dot_general | solution.py:25
  131.4 2.8 %convolution_convert_fusion.4 = bf16[3584,128]{1,0:T(8,128)(2,1)S(1)} fusion(bf16[384,128]{1,0:T(8,128)(2,1)S(1)} %bitcast.169, bf16[384,3712]{1,0:T(8,128)(2,1)} %bitcast.23), kind=kOutput, calls=%fused_computation.14 | convolution fusion | flops 352780288 | bytes 3768320 | tf_op jit(solution)/shard_map/rd,rh->dh/dot_general | solution.py:25
  134.2 1.9 pad_maximum_fusion
  136.2 26.7 %all-to-all-done.3 = bf16[8,48,3712]{2,1,0:T(8,128)(2,1)} async-done(((bf16[8,48,3712]{2,1,0:T(8,128)(2,1)}), bf16[8,48,3712]{2,1,0:T(8,128)(2,1)}, u32[]{:S(2)}, u32[]{:S(2)}) %all-to-all-start.3) | async-done | bytes 2850848 | tf_op jit(solution)/shard_map/all_to_all | solution.py:111
  162.9 3.3 %fusion.7 = bf16[8,8,3712]{2,1,0:T(8,128)(2,1)} fusion(bf16[8,48,3712]{2,1,0:T(8,128)(2,1)} %all-to-all-done.3, bf16[64,48]{0,1:T(8,128)(2,1)S(1)} %fusion.33), kind=kOutput, calls=%fused_computation.17 | convolution fusion | flops 182689792 | bytes 3332096 | tf_op jit(solution)/shard_map/ck,kd->cd/dot_general | solution.py:25
  166.2 8.0 %all-to-all-start.4 = ((bf16[8,8,3712]{2,1,0:T(8,128)(2,1)}), bf16[8,8,3712]{2,1,0:T(8,128)(2,1)S(1)}, u32[]{:S(2)}, u32[]{:S(2)}) async-start(bf16[8,8,3712]{2,1,0:T(8,128)(2,1)} %fusion.7), calls=%async_computation.5 | async-start | bytes 950272 | tf_op jit(solution)/shard_map/all_to_all | solution.py:117
  175.1 1.1 dynamic-slice_bitcast_fusion
  177.7 15.0 %reduce-scatter.2.cloned.1.call-done = bf16[1,3,448,128]{3,2,1,0:T(8,128)(2,1)} async-done(((bf16[8,3,448,128]{3,2,1,0:T(8,128)(2,1)}), bf16[1,3,448,128]{3,2,1,0:T(8,128)(2,1)}) %reduce-scatter.2.cloned.1.call-update) | async-done | bytes 344080 | tf_op jit(solution)/shard_map/reduce_scatter | solution.py:95
  192.7 1.0 convert_element_type.135
  194.7 1.4 convolution_convert_fusion.1
  (54 shorter events, 9.9 us)
Async XLA Ops:
  7.2 4.4 %copy-start = (bf16[128,3584]{1,0:T(8,128)(2,1)S(1)}, bf16[128,3584]{1,0:T(8,128)(2,1)}, u32[]{:S(2)}) copy-start(bf16[128,3584]{1,0:T(8,128)(2,1)} %param.8) | copy-start | bytes 2752516
  7.2 62.0 %all-gather.3.cloned.1.call-start = ((), (), s32[]{:S(2)}) async-start(), calls=%async_computation.6 | async-start | bytes 3096576 | tf_op jit(solution)/shard_map/all_gather | solution.py:32
  14.3 20.9 %all-to-all-start = ((bf16[4,8,7296]{2,1,0:T(8,128)(2,1)}), bf16[4,8,7296]{2,1,0:T(8,128)(2,1)S(1)}, u32[]{:S(2)}, u32[]{:S(2)}) async-start(bf16[4,8,7296]{2,1,0:T(8,128)(2,1)} %maximum_bitcast_fusion), calls=%async_computation | async-start | bytes 933888 | tf_op jit(solution)/shard_map/all_to_all | solution.py:51
  36.3 26.4 %all-to-all-start.1 = ((bf16[4,24,3584]{2,1,0:T(8,128)(2,1)}), bf16[4,24,3584]{2,1,0:T(8,128)(2,1)S(1)}, u32[]{:S(2)}, u32[]{:S(2)}) async-start(bf16[4,24,3584]{2,1,0:T(8,128)(2,1)} %broadcast_in_dim.56), calls=%async_computation.1 | async-start | bytes 1376256 | tf_op jit(solution)/shard_map/all_to_all | solution.py:20
  62.6 1.8 copy-start.2
  64.5 37.1 %all-to-all-start.2 = ((bf16[4,96,3712]{2,1,0:T(8,128)(2,1)}), bf16[4,96,3712]{2,1,0:T(8,128)(2,1)}, u32[]{:S(2)}, u32[]{:S(2)}) async-start(bf16[4,96,3712]{2,1,0:T(8,128)(2,1)} %broadcast_in_dim.64), calls=%async_computation.2 | async-start | bytes 5701632 | tf_op jit(solution)/shard_map/all_to_all | solution.py:20
  69.1 44.7 %all-gather.5.cloned.1.call-start = ((), (), s32[]{:S(2)}) async-start(), calls=%async_computation.7 | async-start | bytes 3440640 | tf_op jit(solution)/shard_map/all_gather | solution.py:65
  116.8 3.9 %copy-start.1 = (bf16[384,3712]{1,0:T(8,128)(2,1)S(1)}, bf16[384,3712]{1,0:T(8,128)(2,1)}, u32[]{:S(2)}) copy-start(bf16[384,3712]{1,0:T(8,128)(2,1)} %fusion.9) | copy-start | bytes 8552452
  124.0 38.9 %all-to-all-start.3 = ((bf16[8,48,3712]{2,1,0:T(8,128)(2,1)}), bf16[8,48,3712]{2,1,0:T(8,128)(2,1)}, u32[]{:S(2)}, u32[]{:S(2)}) async-start(bf16[8,48,3712]{2,1,0:T(8,128)(2,1)} %bitcast.146), calls=%async_computation.4 | async-start | bytes 5701632 | tf_op jit(solution)/shard_map/all_to_all | solution.py:111
  128.4 64.3 %reduce-scatter.2.cloned.1.call-start = ((), (), s32[]{:S(2)}) async-start(), calls=%async_computation.8 | async-start | bytes 3096576 | tf_op jit(solution)/shard_map/reduce_scatter | solution.py:95
  131.4 2.8 %copy-start.3 = (bf16[3584,128]{1,0:T(8,128)(2,1)S(1)}, bf16[3584,128]{1,0:T(8,128)(2,1)}, u32[]{:S(2)}) copy-start(bf16[3584,128]{1,0:T(8,128)(2,1)} %convolution_convert_fusion.3) | copy-start | bytes 2752516
  166.2 28.4 %all-to-all-start.4 = ((bf16[8,8,3712]{2,1,0:T(8,128)(2,1)}), bf16[8,8,3712]{2,1,0:T(8,128)(2,1)S(1)}, u32[]{:S(2)}, u32[]{:S(2)}) async-start(bf16[8,8,3712]{2,1,0:T(8,128)(2,1)} %fusion.7), calls=%async_computation.5 | async-start | bytes 950272 | tf_op jit(solution)/shard_map/all_to_all | solution.py:117
  174.2 22.0 %copy-start.4 = (s32[128,8]{0,1:T(8,128)S(1)}, s32[128,8]{0,1:T(8,128)}, u32[]{:S(2)}) copy-start(s32[128,8]{0,1:T(8,128)} %param.9) | copy-start | bytes 12292
Sparse Core Ops, SparseCore 0:
  10.1 51.8 all-gather.2
  72.0 41.7 all-gather.4
  136.2 56.4 reduce-scatter.1
where the time goes:
time: 204 us; the launch traced here: 203 us
  waiting for transfers between devices  88.8 us (44%)
  starting transfers between devices  35 us (17%)
  matrix products  24.3 us (12%)
  other arithmetic  15.8 us (8%)
  between operations  14 us (7%)
  blocking collectives  12.8 us (6%)
  local copies, waits for them, and re-layouts  12.7 us (6%)
    all_to_all x2, waiting for transfers between devices, spread(): got = lax.all_to_all(copies, axes, split_axis=0, concat_axis=0, tiled=True)  28.3 us
    all_to_all x1, waiting for transfers between devices, shards(): lax.all_to_all(back, ('x', 'zl'), split_axis=0, concat_axis=0, tiled=True)  26.7 us
    dot_general x14, matrix products, dot(): return jnp.einsum(eq, a, b, preferred_element_type=F32)  24.3 us
    reduce_scatter x1, waiting for transfers between devices, shards(): lax.psum_scatter(grads, DP, scatter_dimension=0, tiled=True)[0].astype(F32)  15 us
    all_gather x1, blocking collectives, shards(): tok_half = lax.all_gather(tok_rows, 'x', axis=0, tiled=True)  12.8 us
    all_to_all x2, starting transfers between devices, spread(): got = lax.all_to_all(copies, axes, split_axis=0, concat_axis=0, tiled=True)  12.2 us
    all_to_all x1, waiting for transfers between devices, shards(): rows = lax.all_to_all(rows, 'ex', split_axis=0, concat_axis=0, tiled=True)  10.8 us
    all_to_all x1, starting transfers between devices, shards(): rows = lax.all_to_all(rows, 'ex', split_axis=0, concat_axis=0, tiled=True)  10 us
  transfers between devices with their start and end apart: 8, of which 6 were waited for; matrix products, arithmetic and copies ran while one was open for 19% of the time, Pallas kernels for 0%

commit v1 on v0

--- a/solution.py
+++ b/solution.py
@@ -62,7 +62,9 @@
     cot_half = spread(cot_rows, ("zl", "yl"))
     cot_half, gathered = lax.optimization_barrier((cot_half, gathered))
     slot_all = spread(tok_half, ("zl", "yl"))
-    slot_cotan = lax.all_gather(cot_half, "x", axis=0, tiled=True)
+    slot_cotan = jnp.concatenate(
+        lax.all_to_all(jnp.stack([cot_half] * lax.axis_size("x")), "x", 0, 0), axis=0
+    )
     slot_tokens = slot_all[:, :features]
     gathered = gathered.reshape(n_dp, 3, hidden_dev, features)
 

time: 204 us -> 244 us (1.20)
  the two profiles are of different devices: /device:TPU:17 before, /device:TPU:1 now
where the time goes in v1:
time: 244 us; the launch traced here: 243 us
  waiting for transfers between devices  120 us (49%)
  starting transfers between devices  39 us (16%)
  matrix products  26.1 us (11%)
  local copies, waits for them, and re-layouts  16.2 us (7%)
  other arithmetic  14.7 us (6%)
  between operations  14.4 us (6%)
  blocking collectives  12.2 us (5%)
    all_gather x1, waiting for transfers between devices, shards(): gathered = lax.all_gather(mine, DP, axis=0, tiled=True)  34.5 us
    all_to_all x1, waiting for transfers between devices, shards(): lax.all_to_all(back, ('x', 'zl'), split_axis=0, concat_axis=0, tiled=True)  28.2 us
    dot_general x14, matrix products, dot(): return jnp.einsum(eq, a, b, preferred_element_type=F32)  26.1 us
    all_to_all x2, waiting for transfers between devices, spread(): got = lax.all_to_all(copies, axes, split_axis=0, concat_axis=0, tiled=True)  17.3 us
    all_to_all x1, waiting for transfers between devices, shards(): lax.all_to_all(jnp.stack([cot_half] * lax.axis_size('x')), 'x', 0, 0)  14.8 us
    reduce_scatter x1, waiting for transfers between devices, shards(): lax.psum_scatter(grads, DP, scatter_dimension=0, tiled=True)[0].astype(F32)  14.6 us
    all_to_all x2, starting transfers between devices, spread(): got = lax.all_to_all(copies, axes, split_axis=0, concat_axis=0, tiled=True)  12.2 us
    all_gather x1, blocking collectives, shards(): tok_half = lax.all_gather(tok_rows, 'x', axis=0, tiled=True)  12.2 us
  transfers between devices with their start and end apart: 8, of which 6 were waited for; matrix products, arithmetic and copies ran while one was open for 14% of the time, Pallas kernels for 0%

profile of v1, /device:TPU:1, one launch (start us, length us, event | category | flops | bytes accessed | tf_op | source)
XLA Modules:
  0.0 242.9 jit_solution(1743656335894108593)
XLA Ops:
  10.1 1.5 convolution_convert_fusion.6
  12.5 10.8 %all-to-all-start = ((bf16[4,8,7296]{2,1,0:T(8,128)(2,1)}), bf16[4,8,7296]{2,1,0:T(8,128)(2,1)S(1)}, u32[]{:S(2)}, u32[]{:S(2)}) async-start(bf16[4,8,7296]{2,1,0:T(8,128)(2,1)} %maximum_bitcast_fusion), calls=%async_computation | async-start | bytes 933888 | tf_op jit(solution)/shard_map/all_to_all | solution.py:51
  23.3 10.8 %all-to-all-done = bf16[4,8,7296]{2,1,0:T(8,128)(2,1)S(1)} async-done(((bf16[4,8,7296]{2,1,0:T(8,128)(2,1)}), bf16[4,8,7296]{2,1,0:T(8,128)(2,1)S(1)}, u32[]{:S(2)}, u32[]{:S(2)}) %all-to-all-start) | async-done | bytes 466976 | tf_op jit(solution)/shard_map/all_to_all | solution.py:51
  35.3 7.6 %all-to-all-start.1 = ((bf16[4,24,3584]{2,1,0:T(8,128)(2,1)}), bf16[4,24,3584]{2,1,0:T(8,128)(2,1)S(1)}, u32[]{:S(2)}, u32[]{:S(2)}) async-start(bf16[4,24,3584]{2,1,0:T(8,128)(2,1)} %broadcast_in_dim.56), calls=%async_computation.1 | async-start | bytes 1376256 | tf_op jit(solution)/shard_map/all_to_all | solution.py:20
  43.9 12.2 %all_gather.7 = bf16[96,3712]{1,0:T(8,128)(2,1)S(1)} all-gather(bf16[24,3712]{1,0:T(8,128)(2,1)S(1)} %convolution_convert_fusion.7), channel_id=1, replica_groups=mesh['yh'=4,'core'=2,'ex'=4,'zl'=2,'x'=4,'yl'=2] {'x'}, dimensions={0}, use_global_device_ids=true | all-gather | bytes 890880 | tf_op jit(solution)/shard_map/all_gather | solution.py:61
  56.1 1.8 broadcast_in_dim.64
  57.9 4.6 %all-to-all-start.2 = ((bf16[4,96,3712]{2,1,0:T(8,128)(2,1)}), bf16[4,96,3712]{2,1,0:T(8,128)(2,1)}, u32[]{:S(2)}, u32[]{:S(2)}) async-start(bf16[4,96,3712]{2,1,0:T(8,128)(2,1)} %broadcast_in_dim.64), calls=%async_computation.2 | async-start | bytes 5701632 | tf_op jit(solution)/shard_map/all_to_all | solution.py:20
  62.6 34.5 %all-gather.2.cloned.1.call-done = bf16[384,3584]{1,0:T(8,128)(2,1)} async-done(((bf16[48,3584]{1,0:T(8,128)(2,1)}), bf16[384,3584]{1,0:T(8,128)(2,1)}) %all-gather.2.cloned.1.call-update) | async-done | bytes 2752528 | tf_op jit(solution)/shard_map/all_gather | solution.py:32
  97.1 17.3 %all-to-all-done.2 = bf16[4,96,3712]{2,1,0:T(8,128)(2,1)} async-done(((bf16[4,96,3712]{2,1,0:T(8,128)(2,1)}), bf16[4,96,3712]{2,1,0:T(8,128)(2,1)}, u32[]{:S(2)}, u32[]{:S(2)}) %all-to-all-start.2) | async-done | bytes 2850848 | tf_op jit(solution)/shard_map/all_to_all | solution.py:20
  114.4 1.9 stack.4
  116.2 4.6 %all-to-all-start.3 = ((bf16[4,96,3584]{2,1,0:T(8,128)(2,1)}), bf16[4,96,3584]{2,1,0:T(8,128)(2,1)}, u32[]{:S(2)}, u32[]{:S(2)}) async-start(bf16[4,96,3584]{2,1,0:T(8,128)(2,1)} %stack.4), calls=%async_computation.3 | async-start | bytes 5505024 | tf_op jit(solution)/shard_map/all_to_all | solution.py:66
  120.8 2.8 %fusion.63 = (bf16[8,1,16,3584]{3,2,1,0:T(8,128)(2,1)}, bf16[8,1,16,3584]{3,2,1,0:T(8,128)(2,1)S(1)}, bf16[8,1,16,3584]{3,2,1,0:T(8,128)(2,1)S(1)}) fusion(bf16[8,3,16,3584]{3,2,1,0:T(8,128)(2,1)} %bitcast.159), kind=kLoop, calls=%fused_computation.123 | loop fusion | bytes 5505024 | tf_op jit(solution)/shard_map/slice | solution.py:75
  123.8 6.1 %fusion.9 = bf16[384,3712]{1,0:T(8,128)(2,1)} fusion(bf16[128,128]{1,0:T(8,128)(2,1)S(1)} %broadcast_in_dim.108, bf16[128,3584]{1,0:T(8,128)(2,1)S(1)} %bitcast.156, bf16[128,3584]{1,0:T(8,128)(2,1)S(1)} %bitcast.152), kind=kLoop, calls=%fused_computation.23 | loop fusion | flops 19955712 | bytes 4718592 | tf_op jit(solution)/shard_map/concatenate | solution.py:100
  129.9 3.5 %slice.65 = bf16[384,3584]{1,0:T(8,128)(2,1)} slice(bf16[384,3712]{1,0:T(8,128)(2,1)} %bitcast.23), slice={[0:384], [0:3584]} | slice | bytes 5505024 | tf_op jit(solution)/shard_map/slice | solution.py:68
  133.4 1.0 convert_reduce_fusion
  134.6 2.8 %convolution_bitcast_fusion.1 = f32[4,4,24,128]{3,2,0,1:T(8,128)S(1)} fusion(bf16[4,4,24,3584]{3,2,1,0:T(8,128)(2,1)} %bitcast.150, bf16[128,3584,1,1]{1,0,3,2:T(8,128)(2,1)S(1)} %bitcast.153), kind=kOutput, calls=%fused_computation.25 | convolution fusion | flops 352321536 | bytes 3866624 | tf_op jit(solution)/shard_map/rd,hd->rh/dot_general | solution.py:25
  137.4 0.9 multiply_convert_fusion
  138.5 14.8 %all-to-all-done.3 = bf16[4,96,3584]{2,1,0:T(8,128)(2,1)} async-done(((bf16[4,96,3584]{2,1,0:T(8,128)(2,1)}), bf16[4,96,3584]{2,1,0:T(8,128)(2,1)}, u32[]{:S(2)}, u32[]{:S(2)}) %all-to-all-start.3) | async-done | bytes 2752544 | tf_op jit(solution)/shard_map/all_to_all | solution.py:66
  153.3 2.8 %convolution_convert_fusion.2 = bf16[3584,128]{1,0:T(8,128)(2,1)S(1)} fusion(bf16[384,3584]{1,0:T(8,128)(2,1)} %bitcast.25, bf16[384,128]{1,0:T(8,128)(2,1)S(1)} %bitcast.169), kind=kOutput, calls=%fused_computation.12 | convolution fusion | flops 352780288 | bytes 3768320 | tf_op jit(solution)/shard_map/rd,rh->dh/dot_general | solution.py:25
  156.1 2.7 %multiply_reduce_fusion = (bf16[384]{0:T(512)(128)(2,1)S(1)}, bf16[384,128]{1,0:T(8,128)(2,1)S(1)}, bf16[384,128]{1,0:T(8,128)(2,1)S(1)}) fusion(f32[4,4,24,128]{3,2,1,0:T(8,128)S(1)} %copy.53, f32[4,4,24,128]{3,2,1,0:T(8,128)S(1)} %copy.54, f32[384]{0:T(512)S(1)} %reshape.240, bf16[384,3584]{1,0:T(8,128)(2,1)} %bitcast.25, bf16[128,3584]{1,0:T(8,128)(2,1)S(1)} %bitcast.166), kind=kOutput, calls=%fused_computation.57 | convolution fusion | flops 353255040 | bytes 4262144 | tf_op jit(solution)/shard_map/rd,hd->rh/dot_general | solution.py:25
  158.8 3.9 %convolution_convert_fusion.3 = bf16[3584,128]{1,0:T(8,128)(2,1)} fusion(bf16[384,128]{1,0:T(8,128)(2,1)S(1)} %bitcast.176, bf16[384,3712]{1,0:T(8,128)(2,1)} %bitcast.23), kind=kOutput, calls=%fused_computation.13 | convolution fusion | flops 352780288 | bytes 3768320 | tf_op jit(solution)/shard_map/rd,rh->dh/dot_general | solution.py:25
  162.8 3.2 %convolution_convert_fusion = bf16[384,3712]{1,0:T(8,128)(2,1)} fusion(bf16[384,3712]{1,0:T(8,128)(2,1)S(1)} %copy-done.1, bf16[384,128]{1,0:T(8,128)(2,1)S(1)} %broadcast_in_dim.107, bf16[384,128]{1,0:T(8,128)(2,1)S(1)} %get-tuple-element.52, bf16[384,128]{1,0:T(8,128)(2,1)S(1)} %get-tuple-element.51), kind=kOutput, calls=%fused_computation.10 | convolution fusion | flops 1097023488 | bytes 5996544 | tf_op jit(solution)/shard_map/rh,hd->rd/dot_general | solution.py:25
  166.1 4.4 %all-to-all-start.4 = ((bf16[8,48,3712]{2,1,0:T(8,128)(2,1)}), bf16[8,48,3712]{2,1,0:T(8,128)(2,1)}, u32[]{:S(2)}, u32[]{:S(2)}) async-start(bf16[8,48,3712]{2,1,0:T(8,128)(2,1)} %bitcast.149), calls=%async_computation.5 | async-start | bytes 5701632 | tf_op jit(solution)/shard_map/all_to_all | solution.py:113
  170.7 2.8 %convolution_convert_fusion.4 = bf16[3584,128]{1,0:T(8,128)(2,1)S(1)} fusion(bf16[384,128]{1,0:T(8,128)(2,1)S(1)} %bitcast.175, bf16[384,3712]{1,0:T(8,128)(2,1)} %bitcast.23), kind=kOutput, calls=%fused_computation.14 | convolution fusion | flops 352780288 | bytes 3768320 | tf_op jit(solution)/shard_map/rd,rh->dh/dot_general | solution.py:25
  173.5 1.9 pad_maximum_fusion
  175.5 28.2 %all-to-all-done.4 = bf16[8,48,3712]{2,1,0:T(8,128)(2,1)} async-done(((bf16[8,48,3712]{2,1,0:T(8,128)(2,1)}), bf16[8,48,3712]{2,1,0:T(8,128)(2,1)}, u32[]{:S(2)}, u32[]{:S(2)}) %all-to-all-start.4) | async-done | bytes 2850848 | tf_op jit(solution)/shard_map/all_to_all | solution.py:113
  203.7 3.2 %fusion.7 = bf16[8,8,3712]{2,1,0:T(8,128)(2,1)} fusion(bf16[8,48,3712]{2,1,0:T(8,128)(2,1)} %all-to-all-done.4, bf16[64,48]{0,1:T(8,128)(2,1)S(1)} %fusion.29), kind=kOutput, calls=%fused_computation.17 | convolution fusion | flops 182689792 | bytes 3332096 | tf_op jit(solution)/shard_map/ck,kd->cd/dot_general | solution.py:25
  206.9 6.8 %all-to-all-start.5 = ((bf16[8,8,3712]{2,1,0:T(8,128)(2,1)}), bf16[8,8,3712]{2,1,0:T(8,128)(2,1)S(1)}, u32[]{:S(2)}, u32[]{:S(2)}) async-start(bf16[8,8,3712]{2,1,0:T(8,128)(2,1)} %fusion.7), calls=%async_computation.6 | async-start | bytes 950272 | tf_op jit(solution)/shard_map/all_to_all | solution.py:119
  214.6 1.1 dynamic-slice_bitcast_fusion
  217.2 14.6 %reduce-scatter.2.cloned.1.call-done = bf16[1,3,448,128]{3,2,1,0:T(8,128)(2,1)} async-done(((bf16[8,3,448,128]{3,2,1,0:T(8,128)(2,1)}), bf16[1,3,448,128]{3,2,1,0:T(8,128)(2,1)}) %reduce-scatter.2.cloned.1.call-update) | async-done | bytes 344080 | tf_op jit(solution)/shard_map/reduce_scatter | solution.py:97
  231.9 1.0 convert_element_type.155
  233.9 1.4 convolution_convert_fusion.1
  (65 shorter events, 10.9 us)
Async XLA Ops:
  7.2 2.6 %copy-start = (bf16[128,3584]{1,0:T(8,128)(2,1)S(1)}, bf16[128,3584]{1,0:T(8,128)(2,1)}, u32[]{:S(2)}) copy-start(bf16[128,3584]{1,0:T(8,128)(2,1)} %param.8) | copy-start | bytes 2752516
  10.0 32.8 %copy-start.6 = (bf16[1,3584,16]{1,2,0:T(8,128)(2,1)S(1)}, bf16[1,3584,16]{1,2,0:T(8,128)(2,1)}, u32[]{:S(2)}) copy-start(bf16[1,3584,16]{1,2,0:T(8,128)(2,1)} %param.13) | copy-start | bytes 344068
  10.1 32.8 %copy-start.7 = (bf16[1,3584,16]{1,2,0:T(8,128)(2,1)S(1)}, bf16[1,3584,16]{1,2,0:T(8,128)(2,1)}, u32[]{:S(2)}) copy-start(bf16[1,3584,16]{1,2,0:T(8,128)(2,1)} %param.12) | copy-start | bytes 344068
  10.1 32.8 %copy-start.8 = (bf16[1,3584,16]{1,2,0:T(8,128)(2,1)S(1)}, bf16[1,3584,16]{1,2,0:T(8,128)(2,1)}, u32[]{:S(2)}) copy-start(bf16[1,3584,16]{1,2,0:T(8,128)(2,1)} %param.11) | copy-start | bytes 344068
  12.5 21.7 %all-to-all-start = ((bf16[4,8,7296]{2,1,0:T(8,128)(2,1)}), bf16[4,8,7296]{2,1,0:T(8,128)(2,1)S(1)}, u32[]{:S(2)}, u32[]{:S(2)}) async-start(bf16[4,8,7296]{2,1,0:T(8,128)(2,1)} %maximum_bitcast_fusion), calls=%async_computation | async-start | bytes 933888 | tf_op jit(solution)/shard_map/all_to_all | solution.py:51
  35.3 20.8 %all-to-all-start.1 = ((bf16[4,24,3584]{2,1,0:T(8,128)(2,1)}), bf16[4,24,3584]{2,1,0:T(8,128)(2,1)S(1)}, u32[]{:S(2)}, u32[]{:S(2)}) async-start(bf16[4,24,3584]{2,1,0:T(8,128)(2,1)} %broadcast_in_dim.56), calls=%async_computation.1 | async-start | bytes 1376256 | tf_op jit(solution)/shard_map/all_to_all | solution.py:20
  42.9 54.2 %all-gather.2.cloned.1.call-start = ((), (), s32[]{:S(2)}) async-start(), calls=%async_computation.7 | async-start | bytes 3096576 | tf_op jit(solution)/shard_map/all_gather | solution.py:32
  57.9 56.5 %all-to-all-start.2 = ((bf16[4,96,3712]{2,1,0:T(8,128)(2,1)}), bf16[4,96,3712]{2,1,0:T(8,128)(2,1)}, u32[]{:S(2)}, u32[]{:S(2)}) async-start(bf16[4,96,3712]{2,1,0:T(8,128)(2,1)} %broadcast_in_dim.64), calls=%async_computation.2 | async-start | bytes 5701632 | tf_op jit(solution)/shard_map/all_to_all | solution.py:20
  116.2 37.0 %all-to-all-start.3 = ((bf16[4,96,3584]{2,1,0:T(8,128)(2,1)}), bf16[4,96,3584]{2,1,0:T(8,128)(2,1)}, u32[]{:S(2)}, u32[]{:S(2)}) async-start(bf16[4,96,3584]{2,1,0:T(8,128)(2,1)} %stack.4), calls=%async_computation.3 | async-start | bytes 5505024 | tf_op jit(solution)/shard_map/all_to_all | solution.py:66
  123.7 13.7 %copy-start.3 = (bf16[8,1,16,3584]{3,2,1,0:T(8,128)(2,1)}, bf16[8,1,16,3584]{3,2,1,0:T(8,128)(2,1)S(1)}, u32[]{:S(2)}) copy-start(bf16[8,1,16,3584]{3,2,1,0:T(8,128)(2,1)S(1)} %get-tuple-element.45) | copy-start | bytes 2752516
  134.5 2.8 %copy-start.2 = (bf16[384,3584]{1,0:T(8,128)(2,1)S(1)}, bf16[384,3584]{1,0:T(8,128)(2,1)}, u32[]{:S(2)}) copy-start(bf16[384,3584]{1,0:T(8,128)(2,1)} %slice.65) | copy-start | bytes 8257540
  153.3 2.8 %copy-start.4 = (bf16[8,1,16,3584]{3,2,1,0:T(8,128)(2,1)S(1)}, bf16[8,1,16,3584]{3,2,1,0:T(8,128)(2,1)}, u32[]{:S(2)}) copy-start(bf16[8,1,16,3584]{3,2,1,0:T(8,128)(2,1)} %get-tuple-element.44) | copy-start | bytes 2752516
  158.8 4.0 %copy-start.1 = (bf16[384,3712]{1,0:T(8,128)(2,1)S(1)}, bf16[384,3712]{1,0:T(8,128)(2,1)}, u32[]{:S(2)}) copy-start(bf16[384,3712]{1,0:T(8,128)(2,1)} %fusion.9) | copy-start | bytes 8552452
  166.1 37.6 %all-to-all-start.4 = ((bf16[8,48,3712]{2,1,0:T(8,128)(2,1)}), bf16[8,48,3712]{2,1,0:T(8,128)(2,1)}, u32[]{:S(2)}, u32[]{:S(2)}) async-start(bf16[8,48,3712]{2,1,0:T(8,128)(2,1)} %bitcast.149), calls=%async_computation.5 | async-start | bytes 5701632 | tf_op jit(solution)/shard_map/all_to_all | solution.py:113
  170.5 61.4 %reduce-scatter.2.cloned.1.call-start = ((), (), s32[]{:S(2)}) async-start(), calls=%async_computation.8 | async-start | bytes 3096576 | tf_op jit(solution)/shard_map/reduce_scatter | solution.py:97
  170.7 2.8 %copy-start.5 = (bf16[3584,128]{1,0:T(8,128)(2,1)S(1)}, bf16[3584,128]{1,0:T(8,128)(2,1)}, u32[]{:S(2)}) copy-start(bf16[3584,128]{1,0:T(8,128)(2,1)} %convolution_convert_fusion.3) | copy-start | bytes 2752516
  206.9 26.8 %all-to-all-start.5 = ((bf16[8,8,3712]{2,1,0:T(8,128)(2,1)}), bf16[8,8,3712]{2,1,0:T(8,128)(2,1)S(1)}, u32[]{:S(2)}, u32[]{:S(2)}) async-start(bf16[8,8,3712]{2,1,0:T(8,128)(2,1)} %fusion.7), calls=%async_computation.6 | async-start | bytes 950272 | tf_op jit(solution)/shard_map/all_to_all | solution.py:119
  213.6 21.7 %copy-start.9 = (s32[128,8]{0,1:T(8,128)S(1)}, s32[128,8]{0,1:T(8,128)}, u32[]{:S(2)}) copy-start(s32[128,8]{0,1:T(8,128)} %param.9) | copy-start | bytes 12292
Sparse Core Ops, SparseCore 0:
  45.8 51.2 all-gather.1
  175.5 56.2 reduce-scatter.1
